TPU v7x, 512 devices: a whole 4x8x8 slice. The times are simulated.
512 devices in a mesh: cuts: 4 (over y_hi, core), mode: 128 (over x, y_lo, z).
Axes of the slice: x: 4, y: 8 (y_hi: 2, y_lo: 4; y = y_hi * 4 + y_lo), z: 8, core: 2. Of those that a mesh axis runs over, the one named last changes fastest.
Arguments:
- stem: bfloat16 [4, 2, 1024, 16384], P('cuts', None, None, 'mode'), may hold values from -6 to 6
- branches: bfloat16 [3, 2, 1024, 1024], P(None, None, None, 'mode'), may hold values from -0.125 to 0.125
- order: int32 [3], replicated, may hold values from 0 to 2, each once
- swap_order: int32 [3, 1024], replicated, may hold values from 0 to 1023, each once within a row
- row_bits: int32 [2048], replicated, may hold values from 0 to 1023
- column_bits: int32 [2048], replicated, may hold values from 0 to 16383
Outputs:
- stem_out: bfloat16 [4, 2, 1024, 16384], P('cuts', None, None, 'mode')
- amplitudes: float32 [2, 2048], P(None, ('cuts', 'mode'))
All inputs are finite; a program needn't handle non-finite values.
Results may differ from a plain program's by a relative error of at most 0.009.
Values may be sent and summed in bfloat16 or wider, within the bound.
A program may use at most 128 MiB of HBM per device.

v0:
```python
import jax
import jax.numpy as jnp
from jax import lax
from jax.sharding import Mesh
from jax.sharding import PartitionSpec as P

MODE = ("mode_0", "mode_1", "mode_2")
CUTS_MODE = ("cuts_0", "cuts_1", "mode_0", "mode_1", "mode_2")
CUTS = ("cuts_0", "cuts_1")


def cut_rows(length, count):
    unit = 8 if length >= 8 * count else 1
    return [length // unit * k // count * unit for k in range(1, count)]


def gather_in_order(shard, axes, turns):
    blocks = shard[None]
    for k in turns:
        blocks = lax.all_gather(blocks, axes[k], axis=0, tiled=True)
    held = [lax.axis_size(axes[k]) for k in reversed(turns)]
    blocks = blocks.reshape(*held, *shard.shape)
    turned = sorted(range(len(turns)), key=lambda place: turns[len(turns) - 1 - place])
    return blocks.transpose(*turned, *range(len(turns), blocks.ndim)).reshape(-1, *shard.shape)


def joined_along(blocks, dim):
    blocks = jnp.moveaxis(blocks, 0, dim)
    dims = blocks.shape
    return blocks.reshape(*dims[:dim], dims[dim] * dims[dim + 1], *dims[dim + 2 :])


def gather_at_once(shard, axes, dim):
    cut = max(range(max(1, shard.ndim - 1)), key=lambda d: shard.shape[d])
    count, finished = (len(axes), [])
    for initial, slab in enumerate(jnp.split(shard, cut_rows(shard.shape[cut], count), axis=cut)):
        if slab.size:
            turns = [(initial - k) % count for k in range(count)]
            finished.append(gather_in_order(slab, axes, turns))
    return joined_along(jnp.concatenate(finished, axis=cut + 1), dim)


def over_axes(shard, axes):
    for axis in axes:
        shard = lax.psum(shard, axis)
    return shard


def absorb(matrix, part):
    numbers = (((0,), (0,)), ((), ()))

    def product(left, right):
        return lax.dot_general(left, right, numbers, preferred_element_type=jnp.float32)

    real = product(matrix[0], part[0]) - product(matrix[1], part[1])
    imag = product(matrix[0], part[1]) + product(matrix[1], part[0])
    return jnp.stack([real, imag], axis=0)


def body(stem, branches, order, swap_order, row_bits, column_bits):
    local = stem[0]
    groups = lax.axis_size(MODE)
    width = local.shape[1]
    rows = local.shape[2]
    everything = gather_at_once(branches, MODE, 3)
    for step in range(swap_order.shape[0]):
        moved = jnp.take(local, swap_order[step], axis=1)
        view = moved.reshape(2, groups, width // groups, rows)
        swapped = lax.all_to_all(view, MODE, split_axis=1, concat_axis=1, tiled=True)
        current = swapped.reshape(2, width, rows)
        pick = order[step]
        matrix = lax.dynamic_index_in_dim(everything, pick, 0, keepdims=False)
        local = absorb(matrix, current).astype(jnp.bfloat16)
    offset = lax.axis_index(MODE) * rows
    column_local = column_bits - offset
    inside = jnp.logical_and(column_local >= 0, column_local < rows)
    flat_index = row_bits * rows + jnp.clip(column_local, 0, rows - 1)
    flat = local.reshape(2, width * rows)
    values = jnp.take(flat, flat_index, axis=1).astype(jnp.float32)
    values = jnp.where(inside[None, :], values, jnp.zeros_like(values))
    total_amps = over_axes(values, CUTS_MODE)
    share = values.shape[1] // lax.axis_size(CUTS_MODE)
    amplitudes = lax.dynamic_slice_in_dim(total_amps, lax.axis_index(CUTS_MODE) * share, share, 1)
    return (local[None], amplitudes)


def solution(mesh):
    finer = Mesh(
        mesh.devices.reshape(2, 2, 4, 4, 8), ("cuts_0", "cuts_1", "mode_0", "mode_1", "mode_2")
    )
    placed = (P(CUTS, None, None, MODE), P(None, None, None, MODE), P(), P(), P(), P())
    return jax.shard_map(
        body,
        mesh=finer,
        in_specs=placed,
        out_specs=(P(CUTS, None, None, MODE), P(None, CUTS_MODE)),
        check_vma=False,
    )
```

profile of v0, /device:TPU:4, one launch (start us, length us, event | category | flops | bytes accessed | tf_op | source)
XLA Modules:
  0.0 671.8 jit_solution(10324625984427429543)
XLA Ops:
  8.1 33.4 %all-gather.2 = bf16[24,2,344,8]{2,3,1,0:T(8,128)(2,1)} all-gather(bf16[3,2,344,8]{2,3,1,0:T(8,128)(2,1)S(1)} %get-tuple-element.14), channel_id=4, replica_groups=mesh['cuts_0'=2,'cuts_1'=2,'mode_0'=4,'mode_1'=4,'mode_2'=8] {'mode_2'}, dimensions={0}, use_global_device_ids=true | all-gather | bytes 297216 | tf_op jit(solution)/shard_map/all_gather | solution.py:20
  42.4 10.8 %all-gather = bf16[12,2,336,8]{2,3,1,0:T(8,128)(2,1)S(1)} all-gather(bf16[3,2,336,8]{2,3,1,0:T(8,128)(2,1)S(1)} %split.9), channel_id=2, replica_groups=mesh['cuts_0'=2,'cuts_1'=2,'mode_0'=4,'mode_1'=4,'mode_2'=8] {'mode_0'}, dimensions={0}, use_global_device_ids=true | all-gather | bytes 161280 | tf_op jit(solution)/shard_map/all_gather | solution.py:20
  53.2 29.4 %all_gather.28 = bf16[32,3,2,336,8]{3,4,2,1,0:T(8,128)(2,1)} all-gather(bf16[4,3,2,336,8]{3,4,2,1,0:T(8,128)(2,1)S(1)} %bitcast.161), channel_id=1, replica_groups=mesh['cuts_0'=2,'cuts_1'=2,'mode_0'=4,'mode_1'=4,'mode_2'=8] {'mode_2'}, dimensions={0}, use_global_device_ids=true | all-gather | bytes 1161216 | tf_op jit(solution)/shard_map/all_gather | solution.py:20
  82.6 13.6 %all-gather.1 = bf16[12,2,344,8]{2,3,1,0:T(8,128)(2,1)S(1)} all-gather(bf16[3,2,344,8]{2,3,1,0:T(8,128)(2,1)S(1)} %get-tuple-element.13), channel_id=3, replica_groups=mesh['cuts_0'=2,'cuts_1'=2,'mode_0'=4,'mode_1'=4,'mode_2'=8] {'mode_1'}, dimensions={0}, use_global_device_ids=true | all-gather | bytes 165120 | tf_op jit(solution)/shard_map/all_gather | solution.py:20
  96.3 13.6 %all_gather.31 = bf16[16,3,2,344,8]{3,4,2,1,0:T(8,128)(2,1)} all-gather(bf16[4,3,2,344,8]{3,4,2,1,0:T(8,128)(2,1)S(1)} %bitcast.162), channel_id=1, replica_groups=mesh['cuts_0'=2,'cuts_1'=2,'mode_0'=4,'mode_1'=4,'mode_2'=8] {'mode_0'}, dimensions={0}, use_global_device_ids=true | all-gather | bytes 660480 | tf_op jit(solution)/shard_map/all_gather | solution.py:20
  112.9 3.7 gather_fusion.1
  116.6 3.7 broadcast_select_fusion.2
  121.3 11.7 %all-to-all-start = ((bf16[2,128,8,128]{3,2,0,1:T(8,128)(2,1)}), bf16[2,128,8,128]{3,2,0,1:T(8,128)(2,1)S(1)}, u32[]{:S(2)}, u32[]{:S(2)}) async-start(bf16[2,128,8,128]{3,2,0,1:T(8,128)(2,1)} %copy.45), calls=%async_computation | async-start | bytes 1048576 | tf_op jit(solution)/shard_map/all_to_all | solution.py:69
  136.4 48.8 %all-gather.8.cloned.1.call-done = bf16[128,3,2,336,8]{3,4,2,1,0:T(8,128)(2,1)} async-done(((bf16[32,3,2,336,8]{3,4,2,1,0:T(8,128)(2,1)}), bf16[128,3,2,336,8]{3,4,2,1,0:T(8,128)(2,1)}) %all-gather.8.cloned.1.call-update) | async-done | bytes 4128784 | tf_op jit(solution)/shard_map/all_gather | solution.py:20
  185.1 5.2 copy.41
  190.4 61.7 %all-gather.10.cloned.1.call-done = bf16[128,3,2,344,8]{3,4,2,1,0:T(8,128)(2,1)} async-done(((bf16[16,3,2,344,8]{3,4,2,1,0:T(8,128)(2,1)}), bf16[128,3,2,344,8]{3,4,2,1,0:T(8,128)(2,1)}) %all-gather.10.cloned.1.call-update) | async-done | bytes 4227088 | tf_op jit(solution)/shard_map/all_gather | solution.py:20
  252.0 5.2 copy.42
  257.2 51.9 %all-gather.14.cloned.1.call-done = bf16[128,3,2,344,8]{3,4,2,1,0:T(8,128)(2,1)} async-done(((bf16[32,3,2,344,8]{3,4,2,1,0:T(8,128)(2,1)}), bf16[128,3,2,344,8]{3,4,2,1,0:T(8,128)(2,1)}) %all-gather.14.cloned.1.call-update) | async-done | bytes 4227088 | tf_op jit(solution)/shard_map/all_gather | solution.py:20
  309.1 13.7 %copy_bitcast_fusion = bf16[3,2,1024,1024]{2,3,1,0:T(8,128)(2,1)} fusion(bf16[128,3,2,344,8]{3,4,2,1,0:T(8,128)(2,1)} %all-gather.14.cloned.1.call-done, bf16[128,3,2,344,8]{3,4,2,1,0:T(8,128)(2,1)} %bitcast.153, bf16[128,3,2,336,8]{3,4,2,1,0:T(8,128)(2,1)} %bitcast.152), kind=kLoop, calls=%fused_computation.5 | loop fusion | flops 37748736 | bytes 25165824 | tf_op jit(solution)/shard_map/reshape | solution.py:30
  329.8 2.3 fusion.29
  332.7 3.7 gather_fusion.2
  336.4 3.7 broadcast_select_fusion.1
  341.0 14.8 %all-to-all-start.1 = ((bf16[2,128,8,128]{3,2,0,1:T(8,128)(2,1)}), bf16[2,128,8,128]{3,2,0,1:T(8,128)(2,1)S(1)}, u32[]{:S(2)}, u32[]{:S(2)}) async-start(bf16[2,128,8,128]{3,2,0,1:T(8,128)(2,1)} %copy.49), calls=%async_computation.1 | async-start | bytes 1048576 | tf_op jit(solution)/shard_map/all_to_all | solution.py:69
  357.9 15.8 %all-to-all-done.1 = bf16[2,128,8,128]{3,2,0,1:T(8,128)(2,1)S(1)} async-done(((bf16[2,128,8,128]{3,2,0,1:T(8,128)(2,1)}), bf16[2,128,8,128]{3,2,0,1:T(8,128)(2,1)S(1)}, u32[]{:S(2)}, u32[]{:S(2)}) %all-to-all-start.1) | async-done | bytes 524320 | tf_op jit(solution)/shard_map/all_to_all | solution.py:69
  380.5 2.3 fusion.27
  383.4 3.7 gather_fusion.3
  387.1 3.7 broadcast_select_fusion
  391.8 8.2 %all-to-all-start.2 = ((bf16[2,128,8,128]{3,2,0,1:T(8,128)(2,1)}), bf16[2,128,8,128]{3,2,0,1:T(8,128)(2,1)S(1)}, u32[]{:S(2)}, u32[]{:S(2)}) async-start(bf16[2,128,8,128]{3,2,0,1:T(8,128)(2,1)} %copy.53), calls=%async_computation.2 | async-start | bytes 1048576 | tf_op jit(solution)/shard_map/all_to_all | solution.py:69
  401.9 15.7 %all-to-all-done.2 = bf16[2,128,8,128]{3,2,0,1:T(8,128)(2,1)S(1)} async-done(((bf16[2,128,8,128]{3,2,0,1:T(8,128)(2,1)}), bf16[2,128,8,128]{3,2,0,1:T(8,128)(2,1)S(1)}, u32[]{:S(2)}, u32[]{:S(2)}) %all-to-all-start.2) | async-done | bytes 524320 | tf_op jit(solution)/shard_map/all_to_all | solution.py:69
  424.4 2.3 fusion.25
  429.6 20.3 %copy.56 = bf16[2,131072]{0,1:T(8,128)(2,1)} copy(bf16[2,131072]{1,0:T(2,128)(2,1)S(1)} %pad_maximum_fusion.3) | data formatting | bytes 1048576 | tf_op jit(solution)/shard_map/stack | solution.py:57
  449.8 21.6 %gather_fusion = bf16[2048,2]{1,0:T(8,128)(2,1)S(1)} fusion(bf16[2,131072]{0,1:T(8,128)(2,1)} %copy.56, s32[2048]{0:T(1024)S(1)} %broadcast_clamp_fusion), kind=kCustom, calls=%fused_computation.3 | custom fusion | bytes 24576 | tf_op jit(solution)/shard_map/jit(_take)/gather | solution.py:79
  472.2 28.2 %psum.35 = f32[2,2048]{0,1:T(8,128)S(1)} all-reduce(f32[2,2048]{0,1:T(8,128)S(1)} %select_bitcast_fusion), channel_id=1, replica_groups=mesh['cuts_0'=2,'cuts_1'=2,'mode_0'=4,'mode_1'=4,'mode_2'=8] {'cuts_0'}, use_global_device_ids=true, to_apply=%region_0.0 | all-reduce | flops 4096 | bytes 32768 | tf_op jit(solution)/shard_map/psum | solution.py:45
  500.5 5.7 psum.36
  506.1 44.0 %psum.37 = f32[2,2048]{0,1:T(8,128)S(1)} all-reduce(f32[2,2048]{0,1:T(8,128)S(1)} %psum.36), channel_id=1, replica_groups=mesh['cuts_0'=2,'cuts_1'=2,'mode_0'=4,'mode_1'=4,'mode_2'=8] {'mode_0'}, use_global_device_ids=true, to_apply=%region_2.4 | all-reduce | flops 4096 | bytes 32768 | tf_op jit(solution)/shard_map/psum | solution.py:45
  550.2 53.7 %psum.38 = f32[2,2048]{0,1:T(8,128)S(1)} all-reduce(f32[2,2048]{0,1:T(8,128)S(1)} %psum.37), channel_id=1, replica_groups=mesh['cuts_0'=2,'cuts_1'=2,'mode_0'=4,'mode_1'=4,'mode_2'=8] {'mode_1'}, use_global_device_ids=true, to_apply=%region_3.5 | all-reduce | flops 4096 | bytes 32768 | tf_op jit(solution)/shard_map/psum | solution.py:45
  603.9 60.6 %psum.39 = f32[2,2048]{0,1:T(8,128)S(1)} all-reduce(f32[2,2048]{0,1:T(8,128)S(1)} %psum.38), channel_id=1, replica_groups=mesh['cuts_0'=2,'cuts_1'=2,'mode_0'=4,'mode_1'=4,'mode_2'=8] {'mode_2'}, use_global_device_ids=true, to_apply=%region_4.6 | all-reduce | flops 4096 | bytes 32768 | tf_op jit(solution)/shard_map/psum | solution.py:45
  (49 shorter events, 35.1 us)
Async XLA Ops:
  7.2 102.8 %all-gather.12.cloned.1.call-start = ((), (), s32[]{:S(2)}) async-start(), calls=%async_computation.5 | async-start | bytes 1474560 | tf_op jit(solution)/shard_map/all_gather | solution.py:20
  41.6 143.6 %all-gather.8.cloned.1.call-start = ((), (), s32[]{:S(2)}) async-start(), calls=%async_computation.3 | async-start | bytes 5898240 | tf_op jit(solution)/shard_map/all_gather | solution.py:20
  82.6 169.5 %all-gather.10.cloned.1.call-start = ((), (), s32[]{:S(2)}) async-start(), calls=%async_computation.4 | async-start | bytes 5308416 | tf_op jit(solution)/shard_map/all_gather | solution.py:20
  109.9 199.2 %all-gather.14.cloned.1.call-start = ((), (), s32[]{:S(2)}) async-start(), calls=%async_computation.6 | async-start | bytes 5898240 | tf_op jit(solution)/shard_map/all_gather | solution.py:20
  121.3 201.6 %all-to-all-start = ((bf16[2,128,8,128]{3,2,0,1:T(8,128)(2,1)}), bf16[2,128,8,128]{3,2,0,1:T(8,128)(2,1)S(1)}, u32[]{:S(2)}, u32[]{:S(2)}) async-start(bf16[2,128,8,128]{3,2,0,1:T(8,128)(2,1)} %copy.45), calls=%async_computation | async-start | bytes 1048576 | tf_op jit(solution)/shard_map/all_to_all | solution.py:69
  332.1 69.7 %copy-start = (s32[2048]{0:T(1024)S(1)}, s32[2048]{0:T(1024)}, u32[]{:S(2)}) copy-start(s32[2048]{0:T(1024)} %param.13) | copy-start | bytes 24580
  332.1 69.7 %copy-start.1 = (s32[2048]{0:T(1024)S(1)}, s32[2048]{0:T(1024)}, u32[]{:S(2)}) copy-start(s32[2048]{0:T(1024)} %param.12) | copy-start | bytes 24580
  341.0 32.6 %all-to-all-start.1 = ((bf16[2,128,8,128]{3,2,0,1:T(8,128)(2,1)}), bf16[2,128,8,128]{3,2,0,1:T(8,128)(2,1)S(1)}, u32[]{:S(2)}, u32[]{:S(2)}) async-start(bf16[2,128,8,128]{3,2,0,1:T(8,128)(2,1)} %copy.49), calls=%async_computation.1 | async-start | bytes 1048576 | tf_op jit(solution)/shard_map/all_to_all | solution.py:69
  391.8 25.8 %all-to-all-start.2 = ((bf16[2,128,8,128]{3,2,0,1:T(8,128)(2,1)}), bf16[2,128,8,128]{3,2,0,1:T(8,128)(2,1)S(1)}, u32[]{:S(2)}, u32[]{:S(2)}) async-start(bf16[2,128,8,128]{3,2,0,1:T(8,128)(2,1)} %copy.53), calls=%async_computation.2 | async-start | bytes 1048576 | tf_op jit(solution)/shard_map/all_to_all | solution.py:69
Sparse Core Ops, SparseCore 0:
  41.7 36.6 all-gather.11
  82.7 102.4 all-gather.7
  187.2 64.7 all-gather.9
  254.0 55.1 all-gather.13
where the time goes:
time: 673 us; the launch traced here: 672 us
  blocking collectives  293 us (44%)
  waiting for transfers between devices  194 us (29%)
  local copies, waits for them, and re-layouts  74.1 us (11%)
  starting transfers between devices  34.8 us (5%)
  other arithmetic  27.9 us (4%)
  matrix products  27.6 us (4%)
  between operations  19.9 us (3%)
    psum x5, blocking collectives, over_axes(): shard = lax.psum(shard, axis)  192 us
    all_gather x4, waiting for transfers between devices, gather_in_order(): blocks = lax.all_gather(blocks, axes[k], axis=0, tiled=True)  162 us
    all_gather x5, blocking collectives, gather_in_order(): blocks = lax.all_gather(blocks, axes[k], axis=0, tiled=True)  101 us
    all_to_all x3, starting transfers between devices, body(): lax.all_to_all(view, MODE, split_axis=1, concat_axis=1, tiled=True)  34.7 us
    all_to_all x3, waiting for transfers between devices, body(): lax.all_to_all(view, MODE, split_axis=1, concat_axis=1, tiled=True)  31.4 us
    dot_general x12, matrix products, product(): lax.dot_general(left, right, numbers, preferred_element_type=jnp.float32)  27.6 us
    another operation x4, local copies, waits for them, and re-layouts, absorb(): return jnp.stack([real, imag], axis=0)  22.1 us
    gather x1, local copies, waits for them, and re-layouts, body(): values = jnp.take(flat, flat_index, axis=1).astype(jnp.float32)  21.6 us
  transfers between devices with their start and end apart: 7, of which 5 were waited for; matrix products, arithmetic and copies ran while one was open for 6% of the time, Pallas kernels for 0%

commit v1 on v0

--- a/solution.py
+++ b/solution.py
@@ -17,7 +17,10 @@
 def gather_in_order(shard, axes, turns):
     blocks = shard[None]
     for k in turns:
-        blocks = lax.all_gather(blocks, axes[k], axis=0, tiled=True)
+        buf = axes[k]
+        blocks = jnp.concatenate(
+            lax.all_to_all(jnp.stack([blocks] * lax.axis_size(buf)), buf, 0, 0), 0
+        )
     held = [lax.axis_size(axes[k]) for k in reversed(turns)]
     blocks = blocks.reshape(*held, *shard.shape)
     turned = sorted(range(len(turns)), key=lambda place: turns[len(turns) - 1 - place])

time: 673 us -> 748 us (1.11)
  the two profiles are of different devices: /device:TPU:4 before, /device:TPU:2 now
where the time goes in v1:
time: 748 us; the launch traced here: 746 us
  blocking collectives  448 us (60%)
  waiting for transfers between devices  124 us (17%)
  local copies, waits for them, and re-layouts  71.7 us (10%)
  starting transfers between devices  44.7 us (6%)
  matrix products  27.6 us (4%)
  other arithmetic  23.6 us (3%)
    all_to_all x7, blocking collectives, gather_in_order(): lax.all_to_all(jnp.stack([blocks] * lax.axis_size(buf)), buf, 0, 0)  255 us
    psum x5, blocking collectives, over_axes(): shard = lax.psum(shard, axis)  192 us
    all_to_all x2, waiting for transfers between devices, gather_in_order(): lax.all_to_all(jnp.stack([blocks] * lax.axis_size(buf)), buf, 0, 0)  94.2 us
    all_to_all x3, starting transfers between devices, body(): lax.all_to_all(view, MODE, split_axis=1, concat_axis=1, tiled=True)  30.5 us
    all_to_all x3, waiting for transfers between devices, body(): lax.all_to_all(view, MODE, split_axis=1, concat_axis=1, tiled=True)  29.7 us
    dot_general x12, matrix products, product(): lax.dot_general(left, right, numbers, preferred_element_type=jnp.float32)  27.6 us
    another operation x4, local copies, waits for them, and re-layouts, absorb(): return jnp.stack([real, imag], axis=0)  22.1 us
    gather x1, local copies, waits for them, and re-layouts, body(): values = jnp.take(flat, flat_index, axis=1).astype(jnp.float32)  21.6 us
  transfers between devices with their start and end apart: 5, of which 4 were waited for; matrix products, arithmetic and copies ran while one was open for 4% of the time, Pallas kernels for 0%

profile of v1, /device:TPU:2, one launch (start us, length us, event | category | flops | bytes accessed | tf_op | source)
XLA Modules:
  0.0 746.1 jit_solution(7715536987216209826)
XLA Ops:
  2.1 9.2 %all-to-all-start = ((bf16[4,1,3,2,336,8]{4,5,3,2,1,0:T(8,128)(2,1)}), bf16[4,1,3,2,336,8]{4,5,3,2,1,0:T(8,128)(2,1)S(1)}, u32[]{:S(2)}, u32[]{:S(2)}) async-start(bf16[4,1,3,2,336,8]{4,5,3,2,1,0:T(8,128)(2,1)} %stack.66), calls=%async_computation | async-start | bytes 294912 | tf_op jit(solution)/shard_map/all_to_all | solution.py:22
  12.2 3.7 all-to-all-done
  15.9 9.0 %all_to_all.60 = bf16[4,1,3,2,344,8]{4,5,3,2,1,0:T(8,128)(2,1)S(1)} all-to-all(bf16[4,1,3,2,344,8]{4,5,3,2,1,0:T(8,128)(2,1)S(1)} %stack.69), channel_id=1, replica_groups=mesh['cuts_0'=2,'cuts_1'=2,'mode_0'=4,'mode_1'=4,'mode_2'=8] {'mode_1'}, dimensions={0} | all-to-all | bytes 264192 | tf_op jit(solution)/shard_map/all_to_all | solution.py:22
  24.9 18.9 %all_to_all.61 = bf16[8,1,3,2,344,8]{4,5,3,2,1,0:T(8,128)(2,1)S(1)} all-to-all(bf16[8,1,3,2,344,8]{4,5,3,2,1,0:T(8,128)(2,1)S(1)} %stack.72), channel_id=1, replica_groups=mesh['cuts_0'=2,'cuts_1'=2,'mode_0'=4,'mode_1'=4,'mode_2'=8] {'mode_2'}, dimensions={0} | all-to-all | bytes 528384 | tf_op jit(solution)/shard_map/all_to_all | solution.py:22
  43.9 10.8 %all_to_all.62 = bf16[4,4,3,2,344,8]{4,5,3,2,1,0:T(8,128)(2,1)S(1)} all-to-all(bf16[4,4,3,2,344,8]{4,5,3,2,1,0:T(8,128)(2,1)S(1)} %stack.70), channel_id=1, replica_groups=mesh['cuts_0'=2,'cuts_1'=2,'mode_0'=4,'mode_1'=4,'mode_2'=8] {'mode_0'}, dimensions={0} | all-to-all | bytes 1056768 | tf_op jit(solution)/shard_map/all_to_all | solution.py:22
  54.8 28.9 %all_to_all.63 = bf16[8,4,3,2,336,8]{4,5,3,2,1,0:T(8,128)(2,1)S(1)} all-to-all(bf16[8,4,3,2,336,8]{4,5,3,2,1,0:T(8,128)(2,1)S(1)} %stack.67), channel_id=1, replica_groups=mesh['cuts_0'=2,'cuts_1'=2,'mode_0'=4,'mode_1'=4,'mode_2'=8] {'mode_2'}, dimensions={0} | all-to-all | bytes 2064384 | tf_op jit(solution)/shard_map/all_to_all | solution.py:22
  83.8 24.6 %all_to_all.64 = bf16[4,8,3,2,344,8]{4,5,3,2,1,0:T(8,128)(2,1)S(1)} all-to-all(bf16[4,8,3,2,344,8]{4,5,3,2,1,0:T(8,128)(2,1)S(1)} %stack.73), channel_id=1, replica_groups=mesh['cuts_0'=2,'cuts_1'=2,'mode_0'=4,'mode_1'=4,'mode_2'=8] {'mode_1'}, dimensions={0} | all-to-all | bytes 2113536 | tf_op jit(solution)/shard_map/all_to_all | solution.py:22
  108.8 54.9 %all_to_all.65 = bf16[4,32,3,2,344,8]{4,5,3,2,1,0:T(8,128)(2,1)} all-to-all(bf16[4,32,3,2,344,8]{4,5,3,2,1,0:T(8,128)(2,1)S(1)} %stack.74), channel_id=1, replica_groups=mesh['cuts_0'=2,'cuts_1'=2,'mode_0'=4,'mode_1'=4,'mode_2'=8] {'mode_0'}, dimensions={0} | all-to-all | bytes 8454144 | tf_op jit(solution)/shard_map/all_to_all | solution.py:22
  164.2 108.2 %all_to_all.66 = bf16[8,16,3,2,344,8]{4,5,3,2,1,0:T(8,128)(2,1)} all-to-all(bf16[8,16,3,2,344,8]{4,5,3,2,1,0:T(8,128)(2,1)S(1)} %stack.71), channel_id=1, replica_groups=mesh['cuts_0'=2,'cuts_1'=2,'mode_0'=4,'mode_1'=4,'mode_2'=8] {'mode_2'}, dimensions={0} | all-to-all | bytes 8454144 | tf_op jit(solution)/shard_map/all_to_all | solution.py:22
  274.9 5.1 all-to-all-start.2
  280.6 3.7 gather_fusion.1
  284.3 3.7 broadcast_select_fusion.2
  289.0 90.5 %all-to-all-done.2 = bf16[4,32,3,2,336,8]{4,5,3,2,1,0:T(8,128)(2,1)} async-done(((bf16[4,32,3,2,336,8]{4,5,3,2,1,0:T(8,128)(2,1)}), bf16[4,32,3,2,336,8]{4,5,3,2,1,0:T(8,128)(2,1)}, u32[]{:S(2)}, u32[]{:S(2)}) %all-to-all-start.2) | async-done | bytes 4128800 | tf_op jit(solution)/shard_map/all_to_all | solution.py:22
  379.4 8.3 %all-to-all-start.9 = ((bf16[2,128,8,128]{3,2,0,1:T(8,128)(2,1)}), bf16[2,128,8,128]{3,2,0,1:T(8,128)(2,1)S(1)}, u32[]{:S(2)}, u32[]{:S(2)}) async-start(bf16[2,128,8,128]{3,2,0,1:T(8,128)(2,1)} %copy.37), calls=%async_computation.9 | async-start | bytes 1048576 | tf_op jit(solution)/shard_map/all_to_all | solution.py:72
  390.3 3.2 copy.34
  393.5 3.1 copy.33
  396.7 9.4 %copy_bitcast_fusion = bf16[3,2,1024,1024]{2,3,1,0:T(8,128)(2,1)} fusion(bf16[128,3,2,344,8]{3,4,2,1,0:T(8,128)(2,1)S(1)} %bitcast.158, bf16[128,3,2,344,8]{3,4,2,1,0:T(8,128)(2,1)S(1)} %bitcast.159, bf16[128,3,2,336,8]{3,4,2,1,0:T(8,128)(2,1)S(1)} %bitcast.160), kind=kLoop, calls=%fused_computation.5 | loop fusion | flops 37748736 | bytes 25165824 | tf_op jit(solution)/shard_map/reshape | solution.py:33
  416.0 3.7 gather_fusion.2
  419.7 3.7 broadcast_select_fusion.1
  424.3 14.2 %all-to-all-start.10 = ((bf16[2,128,8,128]{3,2,0,1:T(8,128)(2,1)}), bf16[2,128,8,128]{3,2,0,1:T(8,128)(2,1)S(1)}, u32[]{:S(2)}, u32[]{:S(2)}) async-start(bf16[2,128,8,128]{3,2,0,1:T(8,128)(2,1)} %copy.41), calls=%async_computation.10 | async-start | bytes 1048576 | tf_op jit(solution)/shard_map/all_to_all | solution.py:72
  440.6 13.9 %all-to-all-done.10 = bf16[2,128,8,128]{3,2,0,1:T(8,128)(2,1)S(1)} async-done(((bf16[2,128,8,128]{3,2,0,1:T(8,128)(2,1)}), bf16[2,128,8,128]{3,2,0,1:T(8,128)(2,1)S(1)}, u32[]{:S(2)}, u32[]{:S(2)}) %all-to-all-start.10) | async-done | bytes 524320 | tf_op jit(solution)/shard_map/all_to_all | solution.py:72
  464.3 3.7 gather_fusion.3
  468.0 3.7 broadcast_select_fusion
  472.6 8.1 %all-to-all-start.11 = ((bf16[2,128,8,128]{3,2,0,1:T(8,128)(2,1)}), bf16[2,128,8,128]{3,2,0,1:T(8,128)(2,1)S(1)}, u32[]{:S(2)}, u32[]{:S(2)}) async-start(bf16[2,128,8,128]{3,2,0,1:T(8,128)(2,1)} %copy.45), calls=%async_computation.11 | async-start | bytes 1048576 | tf_op jit(solution)/shard_map/all_to_all | solution.py:72
  482.7 15.8 %all-to-all-done.11 = bf16[2,128,8,128]{3,2,0,1:T(8,128)(2,1)S(1)} async-done(((bf16[2,128,8,128]{3,2,0,1:T(8,128)(2,1)}), bf16[2,128,8,128]{3,2,0,1:T(8,128)(2,1)S(1)}, u32[]{:S(2)}, u32[]{:S(2)}) %all-to-all-start.11) | async-done | bytes 524320 | tf_op jit(solution)/shard_map/all_to_all | solution.py:72
  510.6 20.2 %copy.48 = bf16[2,131072]{0,1:T(8,128)(2,1)} copy(bf16[2,131072]{1,0:T(2,128)(2,1)S(1)} %pad_maximum_fusion.3) | data formatting | bytes 1048576 | tf_op jit(solution)/shard_map/stack | solution.py:60
  530.8 21.6 %gather_fusion = bf16[2048,2]{1,0:T(8,128)(2,1)S(1)} fusion(bf16[2,131072]{0,1:T(8,128)(2,1)} %copy.48, s32[2048]{0:T(1024)S(1)} %broadcast_clamp_fusion), kind=kCustom, calls=%fused_computation.3 | custom fusion | bytes 24576 | tf_op jit(solution)/shard_map/jit(_take)/gather | solution.py:82
  553.1 42.6 %psum.35 = f32[2,2048]{0,1:T(8,128)S(1)} all-reduce(f32[2,2048]{0,1:T(8,128)S(1)} %select_bitcast_fusion), channel_id=1, replica_groups=mesh['cuts_0'=2,'cuts_1'=2,'mode_0'=4,'mode_1'=4,'mode_2'=8] {'cuts_0'}, use_global_device_ids=true, to_apply=%region_0.0 | all-reduce | flops 4096 | bytes 32768 | tf_op jit(solution)/shard_map/psum | solution.py:48
  595.8 5.7 psum.36
  601.5 31.2 %psum.37 = f32[2,2048]{0,1:T(8,128)S(1)} all-reduce(f32[2,2048]{0,1:T(8,128)S(1)} %psum.36), channel_id=1, replica_groups=mesh['cuts_0'=2,'cuts_1'=2,'mode_0'=4,'mode_1'=4,'mode_2'=8] {'mode_0'}, use_global_device_ids=true, to_apply=%region_2.4 | all-reduce | flops 4096 | bytes 32768 | tf_op jit(solution)/shard_map/psum | solution.py:48
  632.6 53.0 %psum.38 = f32[2,2048]{0,1:T(8,128)S(1)} all-reduce(f32[2,2048]{0,1:T(8,128)S(1)} %psum.37), channel_id=1, replica_groups=mesh['cuts_0'=2,'cuts_1'=2,'mode_0'=4,'mode_1'=4,'mode_2'=8] {'mode_1'}, use_global_device_ids=true, to_apply=%region_3.5 | all-reduce | flops 4096 | bytes 32768 | tf_op jit(solution)/shard_map/psum | solution.py:48
  685.6 59.7 %psum.39 = f32[2,2048]{0,1:T(8,128)S(1)} all-reduce(f32[2,2048]{0,1:T(8,128)S(1)} %psum.38), channel_id=1, replica_groups=mesh['cuts_0'=2,'cuts_1'=2,'mode_0'=4,'mode_1'=4,'mode_2'=8] {'mode_2'}, use_global_device_ids=true, to_apply=%region_4.6 | all-reduce | flops 4096 | bytes 32768 | tf_op jit(solution)/shard_map/psum | solution.py:48
  (63 shorter events, 43.0 us)
Async XLA Ops:
  2.1 13.8 %all-to-all-start = ((bf16[4,1,3,2,336,8]{4,5,3,2,1,0:T(8,128)(2,1)}), bf16[4,1,3,2,336,8]{4,5,3,2,1,0:T(8,128)(2,1)S(1)}, u32[]{:S(2)}, u32[]{:S(2)}) async-start(bf16[4,1,3,2,336,8]{4,5,3,2,1,0:T(8,128)(2,1)} %stack.66), calls=%async_computation | async-start | bytes 294912 | tf_op jit(solution)/shard_map/all_to_all | solution.py:22
  274.9 5.1 copy-start
  274.9 5.7 copy-start.3
  274.9 104.5 %all-to-all-start.2 = ((bf16[4,32,3,2,336,8]{4,5,3,2,1,0:T(8,128)(2,1)}), bf16[4,32,3,2,336,8]{4,5,3,2,1,0:T(8,128)(2,1)}, u32[]{:S(2)}, u32[]{:S(2)}) async-start(bf16[4,32,3,2,336,8]{4,5,3,2,1,0:T(8,128)(2,1)} %stack.68), calls=%async_computation.2 | async-start | bytes 9437184 | tf_op jit(solution)/shard_map/all_to_all | solution.py:22
  280.0 107.7 %copy-start.4 = (s32[3]{0:T(128)S(1)}, s32[3]{0:T(128)}, u32[]{:S(2)}) copy-start(s32[3]{0:T(128)} %param.10) | copy-start | bytes 40
  379.4 26.7 %all-to-all-start.9 = ((bf16[2,128,8,128]{3,2,0,1:T(8,128)(2,1)}), bf16[2,128,8,128]{3,2,0,1:T(8,128)(2,1)S(1)}, u32[]{:S(2)}, u32[]{:S(2)}) async-start(bf16[2,128,8,128]{3,2,0,1:T(8,128)(2,1)} %copy.37), calls=%async_computation.9 | async-start | bytes 1048576 | tf_op jit(solution)/shard_map/all_to_all | solution.py:72
  390.3 6.4 slice-start
  393.5 3.2 slice-start.1
  424.3 30.1 %all-to-all-start.10 = ((bf16[2,128,8,128]{3,2,0,1:T(8,128)(2,1)}), bf16[2,128,8,128]{3,2,0,1:T(8,128)(2,1)S(1)}, u32[]{:S(2)}, u32[]{:S(2)}) async-start(bf16[2,128,8,128]{3,2,0,1:T(8,128)(2,1)} %copy.41), calls=%async_computation.10 | async-start | bytes 1048576 | tf_op jit(solution)/shard_map/all_to_all | solution.py:72
  461.3 21.3 %copy-start.1 = (s32[2048]{0:T(1024)S(1)}, s32[2048]{0:T(1024)}, u32[]{:S(2)}) copy-start(s32[2048]{0:T(1024)} %param.13) | copy-start | bytes 24580
  461.4 21.3 %copy-start.2 = (s32[2048]{0:T(1024)S(1)}, s32[2048]{0:T(1024)}, u32[]{:S(2)}) copy-start(s32[2048]{0:T(1024)} %param.12) | copy-start | bytes 24580
  472.6 25.9 %all-to-all-start.11 = ((bf16[2,128,8,128]{3,2,0,1:T(8,128)(2,1)}), bf16[2,128,8,128]{3,2,0,1:T(8,128)(2,1)S(1)}, u32[]{:S(2)}, u32[]{:S(2)}) async-start(bf16[2,128,8,128]{3,2,0,1:T(8,128)(2,1)} %copy.45), calls=%async_computation.11 | async-start | bytes 1048576 | tf_op jit(solution)/shard_map/all_to_all | solution.py:72
